TPU v7x, 32 devices: a whole 2x2x4 slice. The times are simulated.
32 devices in a mesh: dp: 8 (over y, x, core), tensor: 4 (over z).
Axes of the slice: x: 2, y: 2, z: 4, core: 2. Of those that a mesh axis runs over, the one named last changes fastest.
Arguments:
- teacher_input: bfloat16 [8, 1024, 1280], P('dp', 'tensor'), may hold values from -6 to 6
- teacher_upstream: bfloat16 [8, 1024, 1280], P('dp', 'tensor'), may hold values from -6 to 6
- teacher_attn_gain: bfloat16 [1280], P('dp'), may hold values from 0.25 to 1.75
- teacher_attn_shift: bfloat16 [1280], P('dp'), may hold values from -1.75 to 1.75
- teacher_qkv_weight: bfloat16 [3, 1280, 1536], P(None, 'dp', 'tensor'), may hold values from -0.15625 to 0.15625
- teacher_qv_bias: bfloat16 [2, 1536], P(None, 'tensor'), may hold values from -0.625 to 0.625
- teacher_out_weight: bfloat16 [1536, 1280], P('tensor', 'dp'), may hold values from -1.25 to 1.25
- teacher_out_bias: bfloat16 [1280], P('dp'), may hold values from -1.75 to 1.75
- teacher_mlp_gain: bfloat16 [1280], P('dp'), may hold values from 0.25 to 1.75
- teacher_mlp_shift: bfloat16 [1280], P('dp'), may hold values from -1.75 to 1.75
- teacher_fc_weight: bfloat16 [1280, 5120], P('dp', 'tensor'), may hold values from -0.15625 to 0.15625
- teacher_fc_bias: bfloat16 [5120], P('tensor'), may hold values from -1.75 to 1.75
- teacher_proj_weight: bfloat16 [5120, 1280], P('tensor', 'dp'), may hold values from -0.078125 to 0.078125
- teacher_proj_bias: bfloat16 [1280], P('dp'), may hold values from -1.75 to 1.75
- student_input: bfloat16 [8, 1024, 768], P('dp', 'tensor'), may hold values from -6 to 6
- student_upstream: bfloat16 [8, 1024, 768], P('dp', 'tensor'), may hold values from -6 to 6
- student_attn_gain: bfloat16 [768], P('dp'), may hold values from 0.25 to 1.75
- student_attn_shift: bfloat16 [768], P('dp'), may hold values from -1.75 to 1.75
- student_qkv_weight: bfloat16 [3, 768, 768], P(None, 'dp', 'tensor'), may hold values from -0.21875 to 0.21875
- student_qv_bias: bfloat16 [2, 768], P(None, 'tensor'), may hold values from -0.625 to 0.625
- student_out_weight: bfloat16 [768, 768], P('tensor', 'dp'), may hold values from -1.75 to 1.75
- student_out_bias: bfloat16 [768], P('dp'), may hold values from -1.75 to 1.75
- student_mlp_gain: bfloat16 [768], P('dp'), may hold values from 0.25 to 1.75
- student_mlp_shift: bfloat16 [768], P('dp'), may hold values from -1.75 to 1.75
- student_fc_weight: bfloat16 [768, 3072], P('dp', 'tensor'), may hold values from -0.21875 to 0.21875
- student_fc_bias: bfloat16 [3072], P('tensor'), may hold values from -1.75 to 1.75
- student_proj_weight: bfloat16 [3072, 768], P('tensor', 'dp'), may hold values from -0.109375 to 0.109375
- student_proj_bias: bfloat16 [768], P('dp'), may hold values from -1.75 to 1.75
- span_starts: int32 [8], P('dp'), may hold values from 0 to 768, as said below
- head_slots: int32 [24], P('tensor'), may hold values from 0 to 1, as said below
Outputs:
- teacher_output: bfloat16 [8, 1024, 1280], P('dp', 'tensor')
- teacher_input_grad: bfloat16 [8, 1024, 1280], P('dp', 'tensor')
- teacher_attn_gain_grad: float32 [1280], P('dp')
- teacher_attn_shift_grad: float32 [1280], P('dp')
- teacher_qkv_weight_grad: float32 [3, 1280, 1536], P(None, 'dp', 'tensor')
- teacher_qv_bias_grad: float32 [2, 1536], P(None, 'tensor')
- teacher_out_weight_grad: float32 [1536, 1280], P('tensor', 'dp')
- teacher_out_bias_grad: float32 [1280], P('dp')
- teacher_mlp_gain_grad: float32 [1280], P('dp')
- teacher_mlp_shift_grad: float32 [1280], P('dp')
- teacher_fc_weight_grad: float32 [1280, 5120], P('dp', 'tensor')
- teacher_fc_bias_grad: float32 [5120], P('tensor')
- teacher_proj_weight_grad: float32 [5120, 1280], P('tensor', 'dp')
- teacher_proj_bias_grad: float32 [1280], P('dp')
- student_output: bfloat16 [8, 1024, 768], P('dp', 'tensor')
- student_input_grad: bfloat16 [8, 1024, 768], P('dp', 'tensor')
- student_attn_gain_grad: float32 [768], P('dp')
- student_attn_shift_grad: float32 [768], P('dp')
- student_qkv_weight_grad: float32 [3, 768, 768], P(None, 'dp', 'tensor')
- student_qv_bias_grad: float32 [2, 768], P(None, 'tensor')
- student_out_weight_grad: float32 [768, 768], P('tensor', 'dp')
- student_out_bias_grad: float32 [768], P('dp')
- student_mlp_gain_grad: float32 [768], P('dp')
- student_mlp_shift_grad: float32 [768], P('dp')
- student_fc_weight_grad: float32 [768, 3072], P('dp', 'tensor')
- student_fc_bias_grad: float32 [3072], P('tensor')
- student_proj_weight_grad: float32 [3072, 768], P('tensor', 'dp')
- student_proj_bias_grad: float32 [768], P('dp')
Inputs may be any that keep to these rules, and one draw needn't show every extreme that they name: `span_starts`: some sequence starts its span at 0 and some at 768. `head_slots`: exactly 20 of the 24 slots are 1.
All inputs are finite; a program needn't handle non-finite values.
Results may differ from a plain program's by a relative error of at most 0.02.
Values may be sent and summed in bfloat16 or wider, within the bound.
No kernel may reach another device: no remote copies, remote signals or barrier semaphores. Data moves between devices by JAX's collectives and lax.ppermute only.
A program may use at most 256 MiB of HBM per device.

v0:
```python
import jax
import jax.numpy as jnp
from jax import lax
from jax.sharding import PartitionSpec as P

HD = 64
SPAN = 256
epsilon = 1e-05
negative = -1e30


def layer_norm(values, norm_gain, norm_shift):
    center = values - jnp.mean(values, axis=-1, keepdims=True)
    spread = jnp.mean(center * center, axis=-1, keepdims=True)
    return center * lax.rsqrt(spread + epsilon) * norm_gain + norm_shift


def gelu_tanh(values):
    return jax.nn.gelu(values, approximate=True)


def visibility(first_row, block_rows, length, span_start):
    query_pos = first_row + jnp.arange(block_rows, dtype=jnp.int32)
    key_pos = jnp.arange(length, dtype=jnp.int32)
    query_in = (query_pos >= span_start) & (query_pos < span_start + SPAN)
    key_in = (key_pos >= span_start) & (key_pos < span_start + SPAN)
    return (key_pos[None, :] <= query_pos[:, None]) | query_in[:, None] & key_in[None, :]


def block_scores(query_block, key_rows, visible, score_scale):
    scores = (
        jnp.einsum("qhe,khe->hqk", query_block, key_rows, preferred_element_type=jnp.float32)
        * score_scale
    )
    return jnp.where(visible[None], scores, negative)


def attention_forward(query_rows, key_rows, value_rows, span_start, block_rows, score_scale):
    length = query_rows.shape[0]
    results = []
    log_sums = []
    for block_index in range(length // block_rows):
        first_row = block_index * block_rows
        visible = visibility(first_row, block_rows, length, span_start)
        scores = block_scores(
            query_rows[first_row : first_row + block_rows], key_rows, visible, score_scale
        )
        row_peak = jnp.max(scores, axis=-1, keepdims=True)
        raised = jnp.exp(scores - row_peak)
        row_total = jnp.sum(raised, axis=-1, keepdims=True)
        weights = (raised / row_total).astype(jnp.bfloat16)
        results.append(
            jnp.einsum("hqk,khe->qhe", weights, value_rows, preferred_element_type=jnp.float32)
        )
        log_sums.append(row_peak + jnp.log(row_total))
    return (jnp.concatenate(results, axis=0), log_sums)


def attention_backward(
    query_rows, key_rows, value_rows, log_sums, heads_grad, span_start, block_rows, score_scale
):
    length = query_rows.shape[0]
    query_grads = []
    key_grad = jnp.zeros(key_rows.shape, jnp.float32)
    value_grad = jnp.zeros(value_rows.shape, jnp.float32)
    for block_index in range(length // block_rows):
        first_row = block_index * block_rows
        last_row = first_row + block_rows
        visible = visibility(first_row, block_rows, length, span_start)
        scores = block_scores(query_rows[first_row:last_row], key_rows, visible, score_scale)
        probability = jnp.exp(scores - log_sums[block_index])
        grad_block = heads_grad[first_row:last_row]
        value_grad = value_grad + jnp.einsum(
            "hqk,qhe->khe",
            probability.astype(jnp.bfloat16),
            grad_block,
            preferred_element_type=jnp.float32,
        )
        prob_grad = jnp.einsum(
            "qhe,khe->hqk", grad_block, value_rows, preferred_element_type=jnp.float32
        )
        weighted = jnp.sum(probability * prob_grad, axis=-1, keepdims=True)
        score_grad = (probability * (prob_grad - weighted)).astype(jnp.bfloat16)
        query_grads.append(
            jnp.einsum("hqk,khe->qhe", score_grad, key_rows, preferred_element_type=jnp.float32)
            * score_scale
        )
        key_grad = (
            key_grad
            + jnp.einsum(
                "hqk,qhe->khe",
                score_grad,
                query_rows[first_row:last_row],
                preferred_element_type=jnp.float32,
            )
            * score_scale
        )
    return (jnp.concatenate(query_grads, axis=0), key_grad, value_grad)


def gather_rows(normed):
    return lax.all_gather(normed, "tensor", axis=0, tiled=True)


def gather_grads(branch_grad):
    return lax.all_gather(branch_grad, "tensor", axis=0, tiled=True)


def sum_rows(left_rows, right_weight):
    return lax.psum_scatter(
        jnp.dot(left_rows, right_weight, preferred_element_type=jnp.float32).astype(jnp.bfloat16),
        "tensor",
        scatter_dimension=0,
        tiled=True,
    ).astype(jnp.float32)


def back_rows(grad_stack, weight_stack):
    return lax.psum_scatter(
        jnp.einsum(
            "sle,sde->ld", grad_stack, weight_stack, preferred_element_type=jnp.float32
        ).astype(jnp.bfloat16),
        "tensor",
        scatter_dimension=0,
        tiled=True,
    ).astype(jnp.float32)


def run_block(
    inputs,
    upstream,
    attn_gain,
    attn_shift,
    qkv_weight,
    qv_bias,
    out_weight,
    out_bias,
    mlp_gain,
    mlp_shift,
    fc_weight,
    fc_bias,
    proj_weight,
    proj_bias,
    span_start,
    head_keep,
):
    gathered = (
        lax.all_gather(qkv_weight, "dp", axis=1, tiled=True),
        lax.all_gather(out_weight, "dp", axis=1, tiled=True),
        lax.all_gather(fc_weight, "dp", axis=0, tiled=True),
        lax.all_gather(proj_weight, "dp", axis=1, tiled=True),
        lax.all_gather(attn_gain, "dp", axis=0, tiled=True),
        lax.all_gather(attn_shift, "dp", axis=0, tiled=True),
        lax.all_gather(out_bias, "dp", axis=0, tiled=True),
        lax.all_gather(mlp_gain, "dp", axis=0, tiled=True),
        lax.all_gather(mlp_shift, "dp", axis=0, tiled=True),
        lax.all_gather(proj_bias, "dp", axis=0, tiled=True),
    )
    qkv_full, out_full, fc_full, proj_full = (gathered[0], gathered[1], gathered[2], gathered[3])
    gain_one = gathered[4].astype(jnp.float32)
    shift_one = gathered[5].astype(jnp.float32)
    bias_out = gathered[6].astype(jnp.float32)
    gain_two = gathered[7].astype(jnp.float32)
    shift_two = gathered[8].astype(jnp.float32)
    bias_proj = gathered[9].astype(jnp.float32)
    rows_first = inputs[0].astype(jnp.float32)
    normed, norm_back_one = jax.vjp(layer_norm, rows_first, gain_one, shift_one)
    normed_all = gather_rows(normed.astype(jnp.bfloat16))
    projected = jnp.einsum("ld,tde->tle", normed_all, qkv_full, preferred_element_type=jnp.float32)
    bias_pair = qv_bias.astype(jnp.float32)
    length = normed_all.shape[0]
    head_count = head_keep.shape[0]
    head_split = (length, head_count, HD)
    query_rows = (projected[0] + bias_pair[0]).astype(jnp.bfloat16).reshape(head_split)
    key_rows = projected[1].astype(jnp.bfloat16).reshape(head_split)
    value_rows = (projected[2] + bias_pair[1]).astype(jnp.bfloat16).reshape(head_split)
    block_rows = min(512, length)
    score_scale = 1.0 / HD**0.5
    attended, log_sums = attention_forward(
        query_rows, key_rows, value_rows, span_start, block_rows, score_scale
    )
    keep_float = head_keep.astype(jnp.float32)[None, :, None]
    heads_low = (attended * keep_float).astype(jnp.bfloat16).reshape(length, head_count * HD)
    attn_sum = sum_rows(heads_low, out_full)
    middle = rows_first + (attn_sum + bias_out)
    normed_two, norm_back_two = jax.vjp(layer_norm, middle, gain_two, shift_two)
    normed_two_all = gather_rows(normed_two.astype(jnp.bfloat16))
    hidden_pre = jnp.dot(
        normed_two_all, fc_full, preferred_element_type=jnp.float32
    ) + fc_bias.astype(jnp.float32)
    hidden, gelu_back = jax.vjp(gelu_tanh, hidden_pre)
    hidden_low = hidden.astype(jnp.bfloat16)
    mlp_sum = sum_rows(hidden_low, proj_full)
    result = middle + (mlp_sum + bias_proj)
    outputs = result.astype(jnp.bfloat16)[None]
    grad_result = upstream[0].astype(jnp.float32)
    grad_mlp_all = gather_grads(upstream[0])
    proj_bias_grad = jnp.sum(grad_mlp_all, axis=0, dtype=jnp.float32)
    proj_grad = jnp.einsum(
        "lf,ld->fd", hidden_low, grad_mlp_all, preferred_element_type=jnp.float32
    )
    hidden_grad = jnp.einsum(
        "ld,fd->lf", grad_mlp_all, proj_full, preferred_element_type=jnp.float32
    )
    pre_grad = gelu_back(hidden_grad)[0].astype(jnp.bfloat16)
    fc_bias_grad = jnp.sum(pre_grad, axis=0, dtype=jnp.float32)
    fc_grad = jnp.einsum("ld,lf->df", normed_two_all, pre_grad, preferred_element_type=jnp.float32)
    normed_two_grad = back_rows(pre_grad[None], fc_full[None])
    middle_from_norm, gain_two_grad, shift_two_grad = norm_back_two(normed_two_grad)
    middle_grad = grad_result + middle_from_norm
    grad_attn_all = gather_grads(middle_grad.astype(jnp.bfloat16))
    out_bias_grad = jnp.sum(grad_attn_all, axis=0, dtype=jnp.float32)
    out_grad = jnp.einsum("le,ld->ed", heads_low, grad_attn_all, preferred_element_type=jnp.float32)
    heads_grad = (
        jnp.einsum("ld,ed->le", grad_attn_all, out_full, preferred_element_type=jnp.float32)
        .astype(jnp.bfloat16)
        .reshape(head_split)
    )
    heads_grad = heads_grad * head_keep.astype(jnp.bfloat16)[None, :, None]
    query_grad, key_grad, value_grad = attention_backward(
        query_rows, key_rows, value_rows, log_sums, heads_grad, span_start, block_rows, score_scale
    )
    qkv_low = jnp.stack(
        [
            query_grad.reshape(length, head_count * HD),
            key_grad.reshape(length, head_count * HD),
            value_grad.reshape(length, head_count * HD),
        ]
    ).astype(jnp.bfloat16)
    qv_bias_grad = jnp.stack(
        [
            jnp.sum(qkv_low[0], axis=0, dtype=jnp.float32),
            jnp.sum(qkv_low[2], axis=0, dtype=jnp.float32),
        ]
    )
    qkv_grad = jnp.einsum("ld,tle->tde", normed_all, qkv_low, preferred_element_type=jnp.float32)
    normed_grad = back_rows(qkv_low, qkv_full)
    rows_from_norm, gain_one_grad, shift_one_grad = norm_back_one(normed_grad)
    input_grad = (middle_grad + rows_from_norm).astype(jnp.bfloat16)[None]
    norm_sums = lax.psum((gain_one_grad, shift_one_grad, gain_two_grad, shift_two_grad), "tensor")
    matrices = (
        qkv_grad,
        out_grad,
        fc_grad,
        proj_grad,
        norm_sums[0],
        norm_sums[1],
        out_bias_grad,
        norm_sums[2],
        norm_sums[3],
        proj_bias_grad,
    )
    biases = (qv_bias_grad, fc_bias_grad)
    return (outputs, input_grad, matrices, biases)


def arrange(outputs, input_grad, matrices, biases):
    return (
        outputs,
        input_grad,
        matrices[4],
        matrices[5],
        matrices[0],
        biases[0],
        matrices[1],
        matrices[6],
        matrices[7],
        matrices[8],
        matrices[2],
        biases[1],
        matrices[3],
        matrices[9],
    )


def on_device(
    teacher_input,
    teacher_upstream,
    teacher_attn_gain,
    teacher_attn_shift,
    teacher_qkv_weight,
    teacher_qv_bias,
    teacher_out_weight,
    teacher_out_bias,
    teacher_mlp_gain,
    teacher_mlp_shift,
    teacher_fc_weight,
    teacher_fc_bias,
    teacher_proj_weight,
    teacher_proj_bias,
    student_input,
    student_upstream,
    student_attn_gain,
    student_attn_shift,
    student_qkv_weight,
    student_qv_bias,
    student_out_weight,
    student_out_bias,
    student_mlp_gain,
    student_mlp_shift,
    student_fc_weight,
    student_fc_bias,
    student_proj_weight,
    student_proj_bias,
    span_starts,
    head_slots,
):
    span_start = span_starts[0]
    teacher = run_block(
        teacher_input,
        teacher_upstream,
        teacher_attn_gain,
        teacher_attn_shift,
        teacher_qkv_weight,
        teacher_qv_bias,
        teacher_out_weight,
        teacher_out_bias,
        teacher_mlp_gain,
        teacher_mlp_shift,
        teacher_fc_weight,
        teacher_fc_bias,
        teacher_proj_weight,
        teacher_proj_bias,
        span_start,
        head_slots,
    )
    student_keep = jnp.ones((student_qv_bias.shape[1] // HD,), jnp.int32)
    student = run_block(
        student_input,
        student_upstream,
        student_attn_gain,
        student_attn_shift,
        student_qkv_weight,
        student_qv_bias,
        student_out_weight,
        student_out_bias,
        student_mlp_gain,
        student_mlp_shift,
        student_fc_weight,
        student_fc_bias,
        student_proj_weight,
        student_proj_bias,
        span_start,
        student_keep,
    )
    teach_parts = teacher[2]
    learn_parts = student[2]
    summed = (
        lax.psum_scatter(teach_parts[0], "dp", scatter_dimension=1, tiled=True),
        lax.psum_scatter(teach_parts[1], "dp", scatter_dimension=1, tiled=True),
        lax.psum_scatter(teach_parts[2], "dp", scatter_dimension=0, tiled=True),
        lax.psum_scatter(teach_parts[3], "dp", scatter_dimension=1, tiled=True),
        lax.psum_scatter(teach_parts[4], "dp", scatter_dimension=0, tiled=True),
        lax.psum_scatter(teach_parts[5], "dp", scatter_dimension=0, tiled=True),
        lax.psum_scatter(teach_parts[6], "dp", scatter_dimension=0, tiled=True),
        lax.psum_scatter(teach_parts[7], "dp", scatter_dimension=0, tiled=True),
        lax.psum_scatter(teach_parts[8], "dp", scatter_dimension=0, tiled=True),
        lax.psum_scatter(teach_parts[9], "dp", scatter_dimension=0, tiled=True),
        lax.psum_scatter(learn_parts[0], "dp", scatter_dimension=1, tiled=True),
        lax.psum_scatter(learn_parts[1], "dp", scatter_dimension=1, tiled=True),
        lax.psum_scatter(learn_parts[2], "dp", scatter_dimension=0, tiled=True),
        lax.psum_scatter(learn_parts[3], "dp", scatter_dimension=1, tiled=True),
        lax.psum_scatter(learn_parts[4], "dp", scatter_dimension=0, tiled=True),
        lax.psum_scatter(learn_parts[5], "dp", scatter_dimension=0, tiled=True),
        lax.psum_scatter(learn_parts[6], "dp", scatter_dimension=0, tiled=True),
        lax.psum_scatter(learn_parts[7], "dp", scatter_dimension=0, tiled=True),
        lax.psum_scatter(learn_parts[8], "dp", scatter_dimension=0, tiled=True),
        lax.psum_scatter(learn_parts[9], "dp", scatter_dimension=0, tiled=True),
    )
    totals = lax.psum((teacher[3][0], teacher[3][1], student[3][0], student[3][1]), "dp")
    teacher_matrices = summed[0:10]
    student_matrices = summed[10:20]
    teacher_biases = (totals[0], totals[1])
    student_biases = (totals[2], totals[3])
    return arrange(teacher[0], teacher[1], teacher_matrices, teacher_biases) + arrange(
        student[0], student[1], student_matrices, student_biases
    )


def solution(mesh):
    in_specs = (
        P("dp", "tensor", None),
        P("dp", "tensor", None),
        P("dp"),
        P("dp"),
        P(None, "dp", "tensor"),
        P(None, "tensor"),
        P("tensor", "dp"),
        P("dp"),
        P("dp"),
        P("dp"),
        P("dp", "tensor"),
        P("tensor"),
        P("tensor", "dp"),
        P("dp"),
        P("dp", "tensor", None),
        P("dp", "tensor", None),
        P("dp"),
        P("dp"),
        P(None, "dp", "tensor"),
        P(None, "tensor"),
        P("tensor", "dp"),
        P("dp"),
        P("dp"),
        P("dp"),
        P("dp", "tensor"),
        P("tensor"),
        P("tensor", "dp"),
        P("dp"),
        P("dp"),
        P("tensor"),
    )
    out_specs = (
        P("dp", "tensor", None),
        P("dp", "tensor", None),
        P("dp"),
        P("dp"),
        P(None, "dp", "tensor"),
        P(None, "tensor"),
        P("tensor", "dp"),
        P("dp"),
        P("dp"),
        P("dp"),
        P("dp", "tensor"),
        P("tensor"),
        P("tensor", "dp"),
        P("dp"),
        P("dp", "tensor", None),
        P("dp", "tensor", None),
        P("dp"),
        P("dp"),
        P(None, "dp", "tensor"),
        P(None, "tensor"),
        P("tensor", "dp"),
        P("dp"),
        P("dp"),
        P("dp"),
        P("dp", "tensor"),
        P("tensor"),
        P("tensor", "dp"),
        P("dp"),
    )
    return jax.shard_map(
        on_device, mesh=mesh, in_specs=in_specs, out_specs=out_specs, check_vma=False
    )
```

profile of v0, /device:TPU:0, one launch (start us, length us, event | category | flops | bytes accessed | tf_op | source)
XLA Modules:
  0.0 1425.0 jit_solution(5786993439719821327)
XLA Ops:
  22.5 26.5 %all-reduce.27 = (bf16[1280]{0:T(1024)(128)(2,1)}, bf16[1280]{0:T(1024)(128)(2,1)}, bf16[1280]{0:T(1024)(128)(2,1)S(1)}, bf16[1280]{0:T(1024)(128)(2,1)S(1)}, bf...) all-reduce(bf16[1280]{0:T(1024)(128)(2,1)S(1)} %dynamic-update-slic, ...), channel_id=1, replica_groups=mesh['dp'=8,'tensor'=4] {'dp'}, use_global_device_ids=true, to_apply=%add.4 | all-reduce | flops 12288 | bytes 49152
  56.3 10.9 all_gather.88
  67.2 13.4 all_gather.101
  80.7 9.0 all_gather.102
  108.0 35.6 %all-gather.16.cloned.1.call-done = bf16[1024,1280]{1,0:T(8,128)(2,1)} async-done(((bf16[256,1280]{1,0:T(8,128)(2,1)}), bf16[1024,1280]{1,0:T(8,128)(2,1)}) %all-gather.16.cloned.1.call-update) | async-done | bytes 2621456 | tf_op jit(solution)/shard_map/all_gather | solution.py:102
  143.6 32.2 %all-gather.18.cloned.1.call-done = bf16[3,1280,384]{2,1,0:T(8,128)(2,1)} async-done(((bf16[3,160,384]{2,1,0:T(8,128)(2,1)}), bf16[3,1280,384]{2,1,0:T(8,128)(2,1)}) %all-gather.18.cloned.1.call-update) | async-done | bytes 2949136 | tf_op jit(solution)/shard_map/all_gather | solution.py:148
  175.8 6.0 fusion.47
  220.0 46.6 %reduce-scatter.20.cloned.1.call-done = bf16[256,1280]{1,0:T(8,128)(2,1)} async-done(((bf16[1024,1280]{1,0:T(8,128)(2,1)}), bf16[256,1280]{1,0:T(8,128)(2,1)}) %reduce-scatter.20.cloned.1.call-update) | async-done | bytes 655376 | tf_op jit(solution)/shard_map/reduce_scatter | solution.py:110
  273.4 18.7 %all-gather.32.cloned.1.call-done = bf16[768,768]{1,0:T(8,128)(2,1)} async-done(((bf16[96,768]{1,0:T(8,128)(2,1)}), bf16[768,768]{1,0:T(8,128)(2,1)}) %all-gather.32.cloned.1.call-update) | async-done | bytes 1179664 | tf_op jit(solution)/shard_map/all_gather | solution.py:150
  292.1 39.3 %all-gather.30.cloned.1.call-done = bf16[1024,768]{1,0:T(8,128)(2,1)} async-done(((bf16[256,768]{1,0:T(8,128)(2,1)}), bf16[1024,768]{1,0:T(8,128)(2,1)}) %all-gather.30.cloned.1.call-update) | async-done | bytes 1572880 | tf_op jit(solution)/shard_map/all_gather | solution.py:102
  336.2 20.0 %all-gather.34.cloned.1.call-done = bf16[768,768]{0,1:T(8,128)(2,1)} async-done(((bf16[768,96]{0,1:T(8,128)(2,1)}), bf16[768,768]{0,1:T(8,128)(2,1)}) %all-gather.34.cloned.1.call-update) | async-done | bytes 1179664 | tf_op jit(solution)/shard_map/all_gather | solution.py:151
  356.2 38.7 %all-gather.40.cloned.1.call-done = bf16[1,1024,768]{2,1,0:T(8,128)(2,1)} async-done(((bf16[1,256,768]{2,1,0:T(8,128)(2,1)}), bf16[1,1024,768]{2,1,0:T(8,128)(2,1)}) %all-gather.40.cloned.1.call-update) | async-done | bytes 1572880 | tf_op jit(solution)/shard_map/all_gather | solution.py:106
  394.9 6.3 convert_reduce_fusion.4
  405.1 5.5 convolution_convert_fusion.4
  411.0 17.4 %all-gather.22.cloned.1.call-done = bf16[1280,1280]{1,0:T(8,128)(2,1)} async-done(((bf16[160,1280]{1,0:T(8,128)(2,1)}), bf16[1280,1280]{1,0:T(8,128)(2,1)}) %all-gather.22.cloned.1.call-update) | async-done | bytes 3276816 | tf_op jit(solution)/shard_map/all_gather | solution.py:150
  428.4 57.0 %all-gather.20.cloned.1.call-done = bf16[1024,1280]{1,0:T(8,128)(2,1)} async-done(((bf16[256,1280]{1,0:T(8,128)(2,1)}), bf16[1024,1280]{1,0:T(8,128)(2,1)}) %all-gather.20.cloned.1.call-update) | async-done | bytes 2621456 | tf_op jit(solution)/shard_map/all_gather | solution.py:102
  485.4 8.6 fusion.166
  493.9 46.5 %all-gather.38.cloned.1.call-done = bf16[1,1024,1280]{2,1,0:T(8,128)(2,1)} async-done(((bf16[1,256,1280]{2,1,0:T(8,128)(2,1)}), bf16[1,1024,1280]{2,1,0:T(8,128)(2,1)}) %all-gather.38.cloned.1.call-update) | async-done | bytes 2621456 | tf_op jit(solution)/shard_map/all_gather | solution.py:106
  540.4 33.6 %all-gather.24.cloned.1.call-done = bf16[1280,1280]{0,1:T(8,128)(2,1)} async-done(((bf16[1280,160]{0,1:T(8,128)(2,1)}), bf16[1280,1280]{0,1:T(8,128)(2,1)}) %all-gather.24.cloned.1.call-update) | async-done | bytes 3276816 | tf_op jit(solution)/shard_map/all_gather | solution.py:151
  574.0 10.7 convert_reduce_fusion.1
  591.2 9.7 convolution_convert_fusion.2
  601.0 10.4 reduce-scatter.38.cloned.1.call-done
  613.5 34.4 %reduce-scatter.36.cloned.1.call-done = bf16[256,768]{1,0:T(8,128)(2,1)} async-done(((bf16[1024,768]{1,0:T(8,128)(2,1)}), bf16[256,768]{1,0:T(8,128)(2,1)}) %reduce-scatter.36.cloned.1.call-update) | async-done | bytes 393232 | tf_op jit(solution)/shard_map/reduce_scatter | solution.py:110
  652.7 48.5 %reduce-scatter.24.cloned.1.call-done = bf16[256,1280]{1,0:T(8,128)(2,1)} async-done(((bf16[1024,1280]{1,0:T(8,128)(2,1)}), bf16[256,1280]{1,0:T(8,128)(2,1)}) %reduce-scatter.24.cloned.1.call-update) | async-done | bytes 655376 | tf_op jit(solution)/shard_map/reduce_scatter | solution.py:119
  703.5 51.6 %reduce-scatter.22.cloned.1.call-done = bf16[256,1280]{1,0:T(8,128)(2,1)} async-done(((bf16[1024,1280]{1,0:T(8,128)(2,1)}), bf16[256,1280]{1,0:T(8,128)(2,1)}) %reduce-scatter.22.cloned.1.call-update) | async-done | bytes 655376 | tf_op jit(solution)/shard_map/reduce_scatter | solution.py:110
  760.7 33.2 %all-gather.36.cloned.1.call-done = bf16[1024,768]{1,0:T(8,128)(2,1)} async-done(((bf16[256,768]{1,0:T(8,128)(2,1)}), bf16[1024,768]{1,0:T(8,128)(2,1)}) %all-gather.36.cloned.1.call-update) | async-done | bytes 1572880 | tf_op jit(solution)/shard_map/all_gather | solution.py:106
  817.1 5.6 multiply_convert_fusion.2
  839.2 10.6 all-gather.26.cloned.1.call-done
  853.0 6.0 fusion.4
  859.0 9.6 multiply_reduce_fusion
  868.6 6.2 multiply_reduce_fusion.1
  878.3 9.7 multiply_convert_fusion.1
  892.7 6.9 multiply_convert_fusion
  911.0 8.4 convolution_bitcast_fusion
  919.3 9.8 copy.70
  929.2 7.8 bitcast_convert_fusion
  937.1 5.2 fusion.63
  947.4 9.8 fusion.38
  957.3 8.9 fusion.168
  977.5 5.3 fusion.152
  987.0 105.4 %all-reduce.30.cloned.1.call-done = f32[3,1280,384]{2,0,1:T(4,128)} async-done(((f32[3,1280,384]{2,0,1:T(4,128)}), f32[3,1280,384]{2,0,1:T(4,128)}) %all-reduce.30.cloned.1.call-update) | async-done | bytes 5898256
  1094.7 52.2 %reduce-scatter.26.cloned.1.call-done = bf16[256,1280]{1,0:T(8,128)(2,1)} async-done(((bf16[1024,1280]{1,0:T(8,128)(2,1)}), bf16[256,1280]{1,0:T(8,128)(2,1)}) %reduce-scatter.26.cloned.1.call-update) | async-done | bytes 655376 | tf_op jit(solution)/shard_map/reduce_scatter | solution.py:119
  1150.3 25.6 %all-reduce.25 = (f32[1280]{0:T(1024)S(1)}, f32[1280]{0:T(1024)S(1)}, f32[2,384]{1,0:T(2,128)}, f32[1280]{0:T(1024)S(1)}, f32[1280]{0:T(1024)S(1)}, /*index=5*/f...) all-reduce(f32[1280]{0:T(1024)S(1)} %get-tuple-element.86, ...), channel_id=8, replica_groups=mesh['dp'=8,'tensor'=4] {'dp'}, use_global_device_ids=true, to_apply=%region_20.21.clone | all-reduce | flops 15488 | bytes 123904
  1178.9 11.3 all-reduce.26
  1193.0 46.7 %reduce-scatter.42.cloned.1.call-done = f32[96,768]{1,0:T(8,128)} async-done(((f32[768,768]{1,0:T(8,128)}), f32[96,768]{1,0:T(8,128)}) %reduce-scatter.42.cloned.1.call-update) | async-done | bytes 294928 | tf_op jit(solution)/shard_map/reduce_scatter | solution.py:361
  1239.6 66.9 %reduce-scatter.32.cloned.1.call-done = f32[1280,160]{0,1:T(8,128)} async-done(((f32[1280,1280]{0,1:T(8,128)}), f32[1280,160]{0,1:T(8,128)}) %reduce-scatter.32.cloned.1.call-update) | async-done | bytes 819216 | tf_op jit(solution)/shard_map/reduce_scatter | solution.py:352
  1306.5 67.4 %reduce-scatter.30.cloned.1.call-done = f32[160,1280]{1,0:T(8,128)} async-done(((f32[1280,1280]{1,0:T(8,128)}), f32[160,1280]{1,0:T(8,128)}) %reduce-scatter.30.cloned.1.call-update) | async-done | bytes 819216 | tf_op jit(solution)/shard_map/reduce_scatter | solution.py:351
  1374.0 44.3 %reduce-scatter.28.cloned.1.call-done = f32[384,160]{0,1:T(8,128)} async-done(((f32[384,1280]{0,1:T(8,128)}), f32[384,160]{0,1:T(8,128)}) %reduce-scatter.28.cloned.1.call-update) | async-done | bytes 245776 | tf_op jit(solution)/shard_map/reduce_scatter | solution.py:350
  (525 shorter events, 205.6 us)
Async XLA Ops:
  7.3 85.9 %all-gather.28.cloned.1.call-start = ((), (), s32[]{:S(2)}) async-start(), calls=%async_computation.28 | async-start | bytes 1966080 | tf_op jit(solution)/shard_map/all_gather | solution.py:102
  51.0 92.6 %all-gather.16.cloned.1.call-start = ((), (), s32[]{:S(2)}) async-start(), calls=%async_computation.15 | async-start | bytes 3276800 | tf_op jit(solution)/shard_map/all_gather | solution.py:102
  53.9 121.9 %all-gather.18.cloned.1.call-start = ((), (), s32[]{:S(2)}) async-start(), calls=%async_computation.16 | async-start | bytes 3317760 | tf_op jit(solution)/shard_map/all_gather | solution.py:148
  54.7 158.6 %reduce-scatter.34.cloned.1.call-start = ((), (), s32[]{:S(2)}) async-start(), calls=%async_computation.29 | async-start | bytes 1966080 | tf_op jit(solution)/shard_map/reduce_scatter | solution.py:110
  90.0 114.4 %copy-start.107 = (f32[384]{0:T(512)}, f32[384]{0:T(512)S(1)}, u32[]{:S(2)}) copy-start(f32[384]{0:T(512)S(1)} %mul.401) | copy-start | bytes 4612
  105.6 76.2 %copy-start.55 = (bf16[3,64,512]{2,1,0:T(8,128)(2,1)}, bf16[3,64,512]{2,1,0:T(8,128)(2,1)S(1)}, u32[]{:S(2)}) copy-start(bf16[3,64,512]{2,1,0:T(8,128)(2,1)S(1)} %fusion.100) | copy-start | bytes 589828
  107.5 159.1 %reduce-scatter.20.cloned.1.call-start = ((), (), s32[]{:S(2)}) async-start(), calls=%async_computation.17 | async-start | bytes 3276800 | tf_op jit(solution)/shard_map/reduce_scatter | solution.py:110
  208.4 83.7 %all-gather.32.cloned.1.call-start = ((), (), s32[]{:S(2)}) async-start(), calls=%async_computation.31 | async-start | bytes 1327104 | tf_op jit(solution)/shard_map/all_gather | solution.py:150
  209.0 122.3 %all-gather.30.cloned.1.call-start = ((), (), s32[]{:S(2)}) async-start(), calls=%async_computation.30 | async-start | bytes 1966080 | tf_op jit(solution)/shard_map/all_gather | solution.py:102
  217.8 138.4 %all-gather.34.cloned.1.call-start = ((), (), s32[]{:S(2)}) async-start(), calls=%async_computation.32 | async-start | bytes 1327104 | tf_op jit(solution)/shard_map/all_gather | solution.py:151
  218.6 176.3 %all-gather.40.cloned.1.call-start = ((), (), s32[]{:S(2)}) async-start(), calls=%async_computation.40 | async-start | bytes 1966080 | tf_op jit(solution)/shard_map/all_gather | solution.py:106
  219.3 209.1 %all-gather.22.cloned.1.call-start = ((), (), s32[]{:S(2)}) async-start(), calls=%async_computation.19 | async-start | bytes 3686400 | tf_op jit(solution)/shard_map/all_gather | solution.py:150
  219.9 265.5 %all-gather.20.cloned.1.call-start = ((), (), s32[]{:S(2)}) async-start(), calls=%async_computation.18 | async-start | bytes 3276800 | tf_op jit(solution)/shard_map/all_gather | solution.py:102
  271.8 268.6 %all-gather.38.cloned.1.call-start = ((), (), s32[]{:S(2)}) async-start(), calls=%async_computation.39 | async-start | bytes 3276800 | tf_op jit(solution)/shard_map/all_gather | solution.py:106
  272.4 301.6 %all-gather.24.cloned.1.call-start = ((), (), s32[]{:S(2)}) async-start(), calls=%async_computation.20 | async-start | bytes 3686400 | tf_op jit(solution)/shard_map/all_gather | solution.py:151
  273.1 338.3 %reduce-scatter.38.cloned.1.call-start = ((), (), s32[]{:S(2)}) async-start(), calls=%async_computation.34 | async-start | bytes 1966080 | tf_op jit(solution)/shard_map/reduce_scatter | solution.py:119
  273.4 131.6 %copy-start.104 = (f32[768]{0:T(1024)}, f32[768]{0:T(1024)S(1)}, u32[]{:S(2)}) copy-start(f32[768]{0:T(1024)S(1)} %convert_element_type.331) | copy-start | bytes 9220
  405.0 242.9 %reduce-scatter.36.cloned.1.call-start = ((), (), s32[]{:S(2)}) async-start(), calls=%async_computation.33 | async-start | bytes 1966080 | tf_op jit(solution)/shard_map/reduce_scatter | solution.py:110
  410.5 290.6 %reduce-scatter.24.cloned.1.call-start = ((), (), s32[]{:S(2)}) async-start(), calls=%async_computation.22 | async-start | bytes 3276800 | tf_op jit(solution)/shard_map/reduce_scatter | solution.py:119
  411.0 180.2 %copy-start.95 = (f32[1280]{0:T(1024)}, f32[1280]{0:T(1024)S(1)}, u32[]{:S(2)}) copy-start(f32[1280]{0:T(1024)S(1)} %convert_element_type.289) | copy-start | bytes 15364
  591.1 164.0 %reduce-scatter.22.cloned.1.call-start = ((), (), s32[]{:S(2)}) async-start(), calls=%async_computation.21 | async-start | bytes 3276800 | tf_op jit(solution)/shard_map/reduce_scatter | solution.py:110
  601.0 100.2 %copy-start.11 = (bf16[256,1280]{1,0:T(8,128)(2,1)S(1)}, bf16[256,1280]{1,0:T(8,128)(2,1)}, u32[]{:S(2)}) copy-start(bf16[256,1280]{1,0:T(8,128)(2,1)} %reduce-scatter.20.cloned.1.call-done) | copy-start | bytes 1966084
  601.0 193.0 %all-gather.36.cloned.1.call-start = ((), (), s32[]{:S(2)}) async-start(), calls=%async_computation.35 | async-start | bytes 1966080 | tf_op jit(solution)/shard_map/all_gather | solution.py:106
  650.2 107.8 %copy-start.92 = (f32[256]{0:T(256)}, f32[256]{0:T(256)S(1)}, u32[]{:S(2)}) copy-start(f32[256]{0:T(256)S(1)} %negate_multiply_fusion.1) | copy-start | bytes 3076
  652.4 197.4 %all-gather.26.cloned.1.call-start = ((), (), s32[]{:S(2)}) async-start(), calls=%async_computation.23 | async-start | bytes 3276800 | tf_op jit(solution)/shard_map/all_gather | solution.py:106
  760.6 211.8 %reduce-scatter.48.cloned.1.call-start = ((), (), s32[]{:S(2)}) async-start(), calls=%async_computation.42 | async-start | bytes 884736
  817.0 157.1 %reduce-scatter.46.cloned.1.call-start = ((), (), s32[]{:S(2)}) async-start(), calls=%async_computation.41 | async-start | bytes 2211840
  834.9 141.0 %reduce-scatter.40.cloned.1.call-start = ((), (), s32[]{:S(2)}) async-start(), calls=%async_computation.36 | async-start | bytes 1966080 | tf_op jit(solution)/shard_map/reduce_scatter | solution.py:119
  838.9 253.5 %all-reduce.30.cloned.1.call-start = ((), (), s32[]{:S(2)}) async-start(), calls=%async_computation.43 | async-start | bytes 15728640
  929.2 217.7 %reduce-scatter.26.cloned.1.call-start = ((), (), s32[]{:S(2)}) async-start(), calls=%async_computation.24 | async-start | bytes 3276800 | tf_op jit(solution)/shard_map/reduce_scatter | solution.py:119
  937.0 255.9 %reduce-scatter.44.cloned.1.call-start = ((), (), s32[]{:S(2)}) async-start(), calls=%async_computation.38 | async-start | bytes 2654208 | tf_op jit(solution)/shard_map/reduce_scatter | solution.py:362
  942.4 297.3 %reduce-scatter.42.cloned.1.call-start = ((), (), s32[]{:S(2)}) async-start(), calls=%async_computation.37 | async-start | bytes 2654208 | tf_op jit(solution)/shard_map/reduce_scatter | solution.py:361
  947.3 359.2 %reduce-scatter.32.cloned.1.call-start = ((), (), s32[]{:S(2)}) async-start(), calls=%async_computation.27 | async-start | bytes 7372800 | tf_op jit(solution)/shard_map/reduce_scatter | solution.py:352
  957.2 416.7 %reduce-scatter.30.cloned.1.call-start = ((), (), s32[]{:S(2)}) async-start(), calls=%async_computation.26 | async-start | bytes 7372800 | tf_op jit(solution)/shard_map/reduce_scatter | solution.py:351
  966.2 452.1 %reduce-scatter.28.cloned.1.call-start = ((), (), s32[]{:S(2)}) async-start(), calls=%async_computation.25 | async-start | bytes 2211840 | tf_op jit(solution)/shard_map/reduce_scatter | solution.py:350
  986.4 160.4 %copy-start.59 = (f32[1280]{0:T(1024)S(1)}, f32[1280]{0:T(1024)}, u32[]{:S(2)}) copy-start(f32[1280]{0:T(1024)} %copy-done.58) | copy-start | bytes 15364
  986.4 160.4 %copy-start.77 = (f32[256]{0:T(256)S(1)}, f32[256]{0:T(256)}, u32[]{:S(2)}) copy-start(f32[256]{0:T(256)} %copy-done.76) | copy-start | bytes 3076
  986.9 161.6 %copy-start.91 = (f32[256]{0:T(256)S(1)}, f32[256]{0:T(256)}, u32[]{:S(2)}) copy-start(f32[256]{0:T(256)} %copy-done.90) | copy-start | bytes 3076
  986.9 161.6 %copy-start.85 = (f32[256]{0:T(256)S(1)}, f32[256]{0:T(256)}, u32[]{:S(2)}) copy-start(f32[256]{0:T(256)} %copy-done.84) | copy-start | bytes 3076
  986.9 163.4 %copy-start.78 = (f32[1280]{0:T(1024)S(1)}, f32[1280]{0:T(1024)}, u32[]{:S(2)}) copy-start(f32[1280]{0:T(1024)} %get-tuple-element.84) | copy-start | bytes 15364
  986.9 163.4 %copy-start.79 = (f32[1280]{0:T(1024)S(1)}, f32[1280]{0:T(1024)}, u32[]{:S(2)}) copy-start(f32[1280]{0:T(1024)} %get-tuple-element.92) | copy-start | bytes 15364
  986.9 163.4 %copy-start.82 = (f32[768]{0:T(1024)S(1)}, f32[768]{0:T(1024)}, u32[]{:S(2)}) copy-start(f32[768]{0:T(1024)} %get-tuple-element.88) | copy-start | bytes 9220
  986.9 163.4 %copy-start.83 = (f32[768]{0:T(1024)S(1)}, f32[768]{0:T(1024)}, u32[]{:S(2)}) copy-start(f32[768]{0:T(1024)} %get-tuple-element.95) | copy-start | bytes 9220
  986.9 163.4 %copy-start.94 = (f32[1280]{0:T(1024)S(1)}, f32[1280]{0:T(1024)}, u32[]{:S(2)}) copy-start(f32[1280]{0:T(1024)} %get-tuple-element.162) | copy-start | bytes 15364
  986.9 163.4 %copy-start.98 = (f32[768]{0:T(1024)S(1)}, f32[768]{0:T(1024)}, u32[]{:S(2)}) copy-start(f32[768]{0:T(1024)} %get-tuple-element.172) | copy-start | bytes 9220
  987.0 203.3 %copy-start.15 = (f32[256,1280]{1,0:T(8,128)S(1)}, f32[256,1280]{1,0:T(8,128)}, u32[]{:S(2)}) copy-start(f32[256,1280]{1,0:T(8,128)} %copy-done.14) | copy-start | bytes 3932164
  987.0 203.3 %copy-start.24 = (bf16[1,256,1280]{2,1,0:T(8,128)(2,1)S(1)}, bf16[1,256,1280]{2,1,0:T(8,128)(2,1)}, u32[]{:S(2)}) copy-start(bf16[1,256,1280]{2,1,0:T(8,128)(2,1)} %param.31) | copy-start | bytes 1966084
  987.0 203.3 %copy-start.87 = (f32[256]{0:T(256)S(1)}, f32[256]{0:T(256)}, u32[]{:S(2)}) copy-start(f32[256]{0:T(256)} %copy-done.86) | copy-start | bytes 3076
  (116 other events, 1637.2 us)
Sparse Core Ops, SparseCore 0:
  51.1 36.5 all-gather.27
  89.9 53.6 all-gather.15
  145.5 30.2 all-gather.17
  178.0 35.2 reduce-scatter.33
  215.5 51.0 reduce-scatter.19
  268.3 23.7 all-gather.31
  294.2 37.0 all-gather.29
  333.2 22.9 all-gather.33
  357.8 37.0 all-gather.39
  396.6 31.7 all-gather.21
  430.5 54.7 all-gather.19
  486.8 53.5 all-gather.37
  542.3 31.6 all-gather.23
  576.1 35.2 reduce-scatter.37
  613.6 34.2 reduce-scatter.35
  650.1 51.0 reduce-scatter.23
  703.3 51.7 reduce-scatter.21
  757.2 36.7 all-gather.35
  796.1 53.6 all-gather.25
  852.8 33.8 reduce-scatter.47
  890.2 40.2 reduce-scatter.45
  932.9 35.2 reduce-scatter.39
  971.9 120.4 all-reduce.29
  1094.6 52.2 reduce-scatter.25
  1150.8 42.1 reduce-scatter.43
  1197.1 42.4 reduce-scatter.41
  1243.5 62.9 reduce-scatter.31
  1311.0 62.9 reduce-scatter.29
  1378.0 40.2 reduce-scatter.27
where the time goes:
time: 1430 us
  waiting for transfers between devices  967 us (68%)
  matrix products  200 us (14%)
  blocking collectives  96.7 us (7%)
  other arithmetic  80.5 us (6%)
  local copies, waits for them, and re-layouts  57.9 us (4%)
  between operations  19.8 us (1%)
    reduce_scatter x4, waiting for transfers between devices, sum_rows(): lax.psum_scatter(jnp.dot(left_rows, right_weight, preferred_element_type=...  137 us
    all_gather x4, waiting for transfers between devices, gather_rows(): return lax.all_gather(normed, 'tensor', axis=0, tiled=True)  132 us
    all_gather x4, waiting for transfers between devices, gather_grads(): return lax.all_gather(branch_grad, 'tensor', axis=0, tiled=True)  129 us
    reduce_scatter x4, waiting for transfers between devices, back_rows(): lax.psum_scatter(jnp.einsum('sle,sde->ld', grad_stack, weight_stack, pref...  111 us
    unnamed x32, waiting for transfers between devices  110 us
    reduce_scatter x1, waiting for transfers between devices, on_device(): lax.psum_scatter(teach_parts[2], 'dp', scatter_dimension=0, tiled=True)  67.4 us
    reduce_scatter x1, waiting for transfers between devices, on_device(): lax.psum_scatter(teach_parts[3], 'dp', scatter_dimension=1, tiled=True)  66.9 us
    all_gather x2, waiting for transfers between devices, run_block(): lax.all_gather(proj_weight, 'dp', axis=1, tiled=True)  53.6 us
  transfers between devices with their start and end apart: 29, of which 25 were waited for; matrix products, arithmetic and copies ran while one was open for 22% of the time, Pallas kernels for 0%

commit v1 on v0

--- a/solution.py
+++ b/solution.py
@@ -7,6 +7,12 @@
 SPAN = 256
 epsilon = 1e-05
 negative = -1e30
+
+
+def draw_pages_all(m, row_dim):
+    wide_out = list(m.shape[1:])
+    wide_out[row_dim] *= m.shape[0]
+    return jnp.moveaxis(m, 0, row_dim).reshape(wide_out)
 
 
 def layer_norm(values, norm_gain, norm_shift):
@@ -144,10 +150,32 @@
     span_start,
     head_keep,
 ):
+
+    def feed_table(at_axis, field, row_axis):
+        shares = jax.lax.psum(1, axis_name=row_axis)
+        crops = tuple(((dd, (dd + 1) % shares) for dd in range(shares)))
+        block_list = tuple(((j, rr) for rr, j in crops))
+        x_new, x_next = ([], [])
+        for u in tuple(range(shares - 1)):
+            if u % 2 == 0:
+                kept_arr = jax.lax.ppermute(
+                    x_new[-1] if x_new else field, perm=crops, axis_name=row_axis
+                )
+                x_new.append(kept_arr)
+            else:
+                heard = jax.lax.ppermute(x_next[-1] if x_next else field, row_axis, perm=block_list)
+                x_next.append(heard)
+        reply = jnp.stack([*x_new[::-1], field, *x_next], axis=0)
+        big = jax.lax.axis_index(row_axis)
+        k_now = len(x_new)
+        answer = big - k_now
+        reply = reply[(jnp.arange(shares) - answer) % shares]
+        return draw_pages_all(reply, at_axis)
+
     gathered = (
         lax.all_gather(qkv_weight, "dp", axis=1, tiled=True),
         lax.all_gather(out_weight, "dp", axis=1, tiled=True),
-        lax.all_gather(fc_weight, "dp", axis=0, tiled=True),
+        feed_table(0, fc_weight, "dp"),
         lax.all_gather(proj_weight, "dp", axis=1, tiled=True),
         lax.all_gather(attn_gain, "dp", axis=0, tiled=True),
         lax.all_gather(attn_shift, "dp", axis=0, tiled=True),

time: 1430 us -> 1380 us (0.965)
  waiting for transfers between devices: 967 us -> 874 us
  local copies, waits for them, and re-layouts: 57.9 us -> 81.4 us
  starting transfers between devices: 3.09 us -> 18.4 us
    all_gather x4, waiting for transfers between devices: 132 us -> 62.5 us  [gather_rows(): return lax.all_gather(normed, 'tensor', axis=0, tiled=True)]
    ppermute x0 -> x14, waiting for transfers between devices: none -> 44.3 us  [the longest x8 31.7 us: feed_table(): jax.lax.ppermute(x_new[-1] if x_new else field, perm=crops, axis_name=row...]
    all_gather x2 -> x0, waiting for transfers between devices: 36 us -> none  [run_block(): lax.all_gather(fc_weight, 'dp', axis=0, tiled=True)]
    all_gather x2, waiting for transfers between devices: 53.6 us -> 33.6 us  [run_block(): lax.all_gather(proj_weight, 'dp', axis=1, tiled=True)]
    unnamed x316 -> x348, local copies, waits for them, and re-layouts: 42 us -> 57.5 us
    ppermute x0 -> x14, starting transfers between devices: none -> 15.1 us  [the longest x6 14.3 us: feed_table(): jax.lax.ppermute(x_next[-1] if x_next else field, row_axis, perm=block_list)]
    unnamed x32 -> x30, waiting for transfers between devices: 110 us -> 109 us
  transfers between devices with their start and end apart: 29 -> 41, of which waited for: 25 -> 28; matrix products, arithmetic and copies ran while one was open for 22% -> 24% of each run, Pallas kernels for 0% -> 0%
where the time goes in v1:
time: 1380 us; the launch traced here: 1370 us
  waiting for transfers between devices  874 us (63%)
  matrix products  198 us (14%)
  blocking collectives  96.7 us (7%)
  local copies, waits for them, and re-layouts  81.4 us (6%)
  other arithmetic  80.3 us (6%)
  between operations  20.5 us (1%)
  starting transfers between devices  18.4 us (1%)
    reduce_scatter x4, waiting for transfers between devices, sum_rows(): lax.psum_scatter(jnp.dot(left_rows, right_weight, preferred_element_type=...  138 us
    all_gather x4, waiting for transfers between devices, gather_grads(): return lax.all_gather(branch_grad, 'tensor', axis=0, tiled=True)  116 us
    reduce_scatter x4, waiting for transfers between devices, back_rows(): lax.psum_scatter(jnp.einsum('sle,sde->ld', grad_stack, weight_stack, pref...  111 us
    unnamed x30, waiting for transfers between devices  109 us
    reduce_scatter x1, waiting for transfers between devices, on_device(): lax.psum_scatter(teach_parts[2], 'dp', scatter_dimension=0, tiled=True)  67.3 us
    reduce_scatter x1, waiting for transfers between devices, on_device(): lax.psum_scatter(teach_parts[3], 'dp', scatter_dimension=1, tiled=True)  67.1 us
    all_gather x4, waiting for transfers between devices, gather_rows(): return lax.all_gather(normed, 'tensor', axis=0, tiled=True)  62.5 us
    unnamed x348, local copies, waits for them, and re-layouts  57.5 us
  transfers between devices with their start and end apart: 41, of which 28 were waited for; matrix products, arithmetic and copies ran while one was open for 24% of the time, Pallas kernels for 0%

profile of v1, /device:TPU:0, one launch (start us, length us, event | category | flops | bytes accessed | tf_op | source)
XLA Modules:
  0.0 1368.7 jit_solution(9108304256789837599)
XLA Ops:
  22.5 26.5 %all-reduce.27 = (bf16[1280]{0:T(1024)(128)(2,1)}, bf16[1280]{0:T(1024)(128)(2,1)}, bf16[1280]{0:T(1024)(128)(2,1)S(1)}, bf16[1280]{0:T(1024)(128)(2,1)S(1)}, bf...) all-reduce(bf16[1280]{0:T(1024)(128)(2,1)S(1)} %dynamic-update-slic, ...), channel_id=1, replica_groups=mesh['dp'=8,'tensor'=4] {'dp'}, use_global_device_ids=true, to_apply=%add.4 | all-reduce | flops 12288 | bytes 49152
  56.3 10.9 all_gather.82
  67.2 13.4 all_gather.94
  80.7 9.0 all_gather.95
  108.0 35.6 %all-gather.14.cloned.1.call-done = bf16[1024,1280]{1,0:T(8,128)(2,1)} async-done(((bf16[256,1280]{1,0:T(8,128)(2,1)}), bf16[1024,1280]{1,0:T(8,128)(2,1)}) %all-gather.14.cloned.1.call-update) | async-done | bytes 2621456 | tf_op jit(solution)/shard_map/all_gather | solution.py:108
  143.7 32.2 %all-gather.16.cloned.1.call-done = bf16[3,1280,384]{2,1,0:T(8,128)(2,1)} async-done(((bf16[3,160,384]{2,1,0:T(8,128)(2,1)}), bf16[3,1280,384]{2,1,0:T(8,128)(2,1)}) %all-gather.16.cloned.1.call-update) | async-done | bytes 2949136 | tf_op jit(solution)/shard_map/all_gather | solution.py:176
  175.9 6.0 fusion.47
  219.5 47.1 %reduce-scatter.20.cloned.1.call-done = bf16[256,1280]{1,0:T(8,128)(2,1)} async-done(((bf16[1024,1280]{1,0:T(8,128)(2,1)}), bf16[256,1280]{1,0:T(8,128)(2,1)}) %reduce-scatter.20.cloned.1.call-update) | async-done | bytes 655376 | tf_op jit(solution)/shard_map/reduce_scatter | solution.py:116
  273.3 5.5 collective-permute-done.7
  284.8 8.5 collective-permute-done.11
  309.4 5.3 collective-permute-done.1
  316.6 6.6 collective-permute-done.2
  327.7 11.5 collective-permute-done.3
  346.0 26.8 %all-gather.34.cloned.1.call-done = bf16[1,1024,768]{2,1,0:T(8,128)(2,1)} async-done(((bf16[1,256,768]{2,1,0:T(8,128)(2,1)}), bf16[1,1024,768]{2,1,0:T(8,128)(2,1)}) %all-gather.34.cloned.1.call-update) | async-done | bytes 1572880 | tf_op jit(solution)/shard_map/all_gather | solution.py:112
  372.8 6.3 convert_reduce_fusion.4
  401.8 26.8 %all-gather.18.cloned.1.call-done = bf16[1024,1280]{1,0:T(8,128)(2,1)} async-done(((bf16[256,1280]{1,0:T(8,128)(2,1)}), bf16[1024,1280]{1,0:T(8,128)(2,1)}) %all-gather.18.cloned.1.call-update) | async-done | bytes 2621456 | tf_op jit(solution)/shard_map/all_gather | solution.py:108
  428.7 8.6 fusion.168
  437.2 46.5 %all-gather.32.cloned.1.call-done = bf16[1,1024,1280]{2,1,0:T(8,128)(2,1)} async-done(((bf16[1,256,1280]{2,1,0:T(8,128)(2,1)}), bf16[1,1024,1280]{2,1,0:T(8,128)(2,1)}) %all-gather.32.cloned.1.call-update) | async-done | bytes 2621456 | tf_op jit(solution)/shard_map/all_gather | solution.py:112
  483.7 33.6 %all-gather.20.cloned.1.call-done = bf16[1280,1280]{0,1:T(8,128)(2,1)} async-done(((bf16[1280,160]{0,1:T(8,128)(2,1)}), bf16[1280,1280]{0,1:T(8,128)(2,1)}) %all-gather.20.cloned.1.call-update) | async-done | bytes 3276816 | tf_op jit(solution)/shard_map/all_gather | solution.py:179
  517.3 10.7 convert_reduce_fusion.1
  534.5 9.8 convolution_convert_fusion.2
  544.5 10.2 reduce-scatter.38.cloned.1.call-done
  556.8 34.6 %reduce-scatter.36.cloned.1.call-done = bf16[256,768]{1,0:T(8,128)(2,1)} async-done(((bf16[1024,768]{1,0:T(8,128)(2,1)}), bf16[256,768]{1,0:T(8,128)(2,1)}) %reduce-scatter.36.cloned.1.call-update) | async-done | bytes 393232 | tf_op jit(solution)/shard_map/reduce_scatter | solution.py:116
  596.0 48.7 %reduce-scatter.24.cloned.1.call-done = bf16[256,1280]{1,0:T(8,128)(2,1)} async-done(((bf16[1024,1280]{1,0:T(8,128)(2,1)}), bf16[256,1280]{1,0:T(8,128)(2,1)}) %reduce-scatter.24.cloned.1.call-update) | async-done | bytes 655376 | tf_op jit(solution)/shard_map/reduce_scatter | solution.py:125
  647.0 51.6 %reduce-scatter.22.cloned.1.call-done = bf16[256,1280]{1,0:T(8,128)(2,1)} async-done(((bf16[1024,1280]{1,0:T(8,128)(2,1)}), bf16[256,1280]{1,0:T(8,128)(2,1)}) %reduce-scatter.22.cloned.1.call-update) | async-done | bytes 655376 | tf_op jit(solution)/shard_map/reduce_scatter | solution.py:116
  704.2 33.2 %all-gather.30.cloned.1.call-done = bf16[1024,768]{1,0:T(8,128)(2,1)} async-done(((bf16[256,768]{1,0:T(8,128)(2,1)}), bf16[1024,768]{1,0:T(8,128)(2,1)}) %all-gather.30.cloned.1.call-update) | async-done | bytes 1572880 | tf_op jit(solution)/shard_map/all_gather | solution.py:112
  760.7 5.6 multiply_convert_fusion.2
  783.2 10.0 all-gather.22.cloned.1.call-done
  796.3 6.0 fusion.4
  802.3 9.6 multiply_reduce_fusion
  811.9 6.3 multiply_reduce_fusion.1
  821.7 9.7 multiply_convert_fusion.1
  836.0 6.7 multiply_convert_fusion
  854.1 8.4 convolution_bitcast_fusion
  862.5 9.8 copy.70
  872.4 7.8 bitcast_convert_fusion
  880.3 5.3 fusion.63
  890.8 9.8 fusion.38
  900.7 8.9 fusion.170
  920.9 5.2 fusion.154
  930.3 105.2 %all-reduce.30.cloned.1.call-done = f32[3,1280,384]{2,0,1:T(4,128)} async-done(((f32[3,1280,384]{2,0,1:T(4,128)}), f32[3,1280,384]{2,0,1:T(4,128)}) %all-reduce.30.cloned.1.call-update) | async-done | bytes 5898256
  1037.8 52.3 %reduce-scatter.26.cloned.1.call-done = bf16[256,1280]{1,0:T(8,128)(2,1)} async-done(((bf16[1024,1280]{1,0:T(8,128)(2,1)}), bf16[256,1280]{1,0:T(8,128)(2,1)}) %reduce-scatter.26.cloned.1.call-update) | async-done | bytes 655376 | tf_op jit(solution)/shard_map/reduce_scatter | solution.py:125
  1093.6 25.6 %all-reduce.25 = (f32[1280]{0:T(1024)S(1)}, f32[1280]{0:T(1024)S(1)}, f32[2,384]{1,0:T(2,128)}, f32[1280]{0:T(1024)S(1)}, f32[1280]{0:T(1024)S(1)}, /*index=5*/f...) all-reduce(f32[1280]{0:T(1024)S(1)} %get-tuple-element.86, ...), channel_id=8, replica_groups=mesh['dp'=8,'tensor'=4] {'dp'}, use_global_device_ids=true, to_apply=%region_20.21.clone | all-reduce | flops 15488 | bytes 123904
  1122.2 11.3 all-reduce.26
  1136.2 46.7 %reduce-scatter.42.cloned.1.call-done = f32[96,768]{1,0:T(8,128)} async-done(((f32[768,768]{1,0:T(8,128)}), f32[96,768]{1,0:T(8,128)}) %reduce-scatter.42.cloned.1.call-update) | async-done | bytes 294928 | tf_op jit(solution)/shard_map/reduce_scatter | solution.py:389
  1182.9 67.1 %reduce-scatter.32.cloned.1.call-done = f32[1280,160]{0,1:T(8,128)} async-done(((f32[1280,1280]{0,1:T(8,128)}), f32[1280,160]{0,1:T(8,128)}) %reduce-scatter.32.cloned.1.call-update) | async-done | bytes 819216 | tf_op jit(solution)/shard_map/reduce_scatter | solution.py:380
  1250.0 67.3 %reduce-scatter.30.cloned.1.call-done = f32[160,1280]{1,0:T(8,128)} async-done(((f32[1280,1280]{1,0:T(8,128)}), f32[160,1280]{1,0:T(8,128)}) %reduce-scatter.30.cloned.1.call-update) | async-done | bytes 819216 | tf_op jit(solution)/shard_map/reduce_scatter | solution.py:379
  1317.2 44.1 %reduce-scatter.28.cloned.1.call-done = f32[384,160]{0,1:T(8,128)} async-done(((f32[384,1280]{0,1:T(8,128)}), f32[384,160]{0,1:T(8,128)}) %reduce-scatter.28.cloned.1.call-update) | async-done | bytes 245776 | tf_op jit(solution)/shard_map/reduce_scatter | solution.py:378
  (585 shorter events, 254.3 us)
Async XLA Ops:
  7.3 85.9 %all-gather.24.cloned.1.call-start = ((), (), s32[]{:S(2)}) async-start(), calls=%async_computation.27 | async-start | bytes 1966080 | tf_op jit(solution)/shard_map/all_gather | solution.py:108
  51.0 92.6 %all-gather.14.cloned.1.call-start = ((), (), s32[]{:S(2)}) async-start(), calls=%async_computation.15 | async-start | bytes 3276800 | tf_op jit(solution)/shard_map/all_gather | solution.py:108
  54.0 121.9 %all-gather.16.cloned.1.call-start = ((), (), s32[]{:S(2)}) async-start(), calls=%async_computation.16 | async-start | bytes 3317760 | tf_op jit(solution)/shard_map/all_gather | solution.py:176
  54.7 158.6 %reduce-scatter.34.cloned.1.call-start = ((), (), s32[]{:S(2)}) async-start(), calls=%async_computation.28 | async-start | bytes 1966080 | tf_op jit(solution)/shard_map/reduce_scatter | solution.py:116
  107.5 159.1 %reduce-scatter.20.cloned.1.call-start = ((), (), s32[]{:S(2)}) async-start(), calls=%async_computation.17 | async-start | bytes 3276800 | tf_op jit(solution)/shard_map/reduce_scatter | solution.py:116
  208.4 132.6 %all-gather.26.cloned.1.call-start = ((), (), s32[]{:S(2)}) async-start(), calls=%async_computation.29 | async-start | bytes 1966080 | tf_op jit(solution)/shard_map/all_gather | solution.py:108
  217.8 128.2 %all-gather.28.cloned.1.call-start = ((), (), s32[]{:S(2)}) async-start(), calls=%async_computation.30 | async-start | bytes 1327104 | tf_op jit(solution)/shard_map/all_gather | solution.py:179
  218.6 154.3 %all-gather.34.cloned.1.call-start = ((), (), s32[]{:S(2)}) async-start(), calls=%async_computation.38 | async-start | bytes 1966080 | tf_op jit(solution)/shard_map/all_gather | solution.py:112
  219.3 209.4 %all-gather.18.cloned.1.call-start = ((), (), s32[]{:S(2)}) async-start(), calls=%async_computation.18 | async-start | bytes 3276800 | tf_op jit(solution)/shard_map/all_gather | solution.py:108
  271.8 211.9 %all-gather.32.cloned.1.call-start = ((), (), s32[]{:S(2)}) async-start(), calls=%async_computation.37 | async-start | bytes 3276800 | tf_op jit(solution)/shard_map/all_gather | solution.py:112
  272.4 244.9 %all-gather.20.cloned.1.call-start = ((), (), s32[]{:S(2)}) async-start(), calls=%async_computation.19 | async-start | bytes 3686400 | tf_op jit(solution)/shard_map/all_gather | solution.py:179
  273.1 281.6 %reduce-scatter.38.cloned.1.call-start = ((), (), s32[]{:S(2)}) async-start(), calls=%async_computation.32 | async-start | bytes 1966080 | tf_op jit(solution)/shard_map/reduce_scatter | solution.py:125
  273.2 5.5 collective-permute-start.7
  278.7 6.1 collective-permute-start.8
  278.7 25.2 %collective-permute-start = (bf16[160,1280]{1,0:T(8,128)(2,1)S(1)}, bf16[160,1280]{1,0:T(8,128)(2,1)}, u32[]{:S(2)}, u32[]{:S(2)}) collective-permute-start(bf16[160,1280]{1,0:T(8,128)(2,1)S(1)} %copy-done.60), channel_id=1, source_target_pairs={{0,4},{4,8},{8,12},{12,16},{16,20},{20,24},{24,28},{28,0},{1,5},{5... | collective-permute-start | bytes 1228808 | tf_op jit(solution)/shard_map/ppermute | solution.py:161
  279.4 24.5 %collective-permute-start.4 = (bf16[160,1280]{1,0:T(8,128)(2,1)S(1)}, bf16[160,1280]{1,0:T(8,128)(2,1)S(1)}, u32[]{:S(2)}, u32[]{:S(2)}) collective-permute-start(bf16[160,1280]{1,0:T(8,128)(2,1)S(1)} %copy-done.60), channel_id=1, source_target_pairs={{4,0},{8,4},{12,8},{16,12},{20,16},{24,20},{28,24},{0,28},{5,1},{9... | collective-permute-start | bytes 1228808 | tf_op jit(solution)/shard_map/ppermute | solution.py:166
  281.4 11.9 collective-permute-start.11
  284.8 11.7 collective-permute-start.9
  293.3 7.4 collective-permute-start.12
  296.5 10.1 collective-permute-start.10
  296.6 237.9 %copy-start.104 = (f32[1280]{0:T(1024)}, f32[1280]{0:T(1024)S(1)}, u32[]{:S(2)}) copy-start(f32[1280]{0:T(1024)S(1)} %convert_element_type.289) | copy-start | bytes 15364
  300.7 22.5 %collective-permute-start.13 = (bf16[96,768]{1,0:T(8,128)(2,1)S(1)}, bf16[96,768]{1,0:T(8,128)(2,1)S(1)}, u32[]{:S(2)}, u32[]{:S(2)}) collective-permute-start(bf16[96,768]{1,0:T(8,128)(2,1)S(1)} %collective-permute-done.12), channel_id=1, source_target_pairs={{4,0},{8,4},{12,8},{16,12},{20,16},{24,20},{28,24},{0,28},{5,1},{9... | collective-permute-start | bytes 442376 | tf_op jit(solution)/shard_map/ppermute | solution.py:166
  303.9 10.7 collective-permute-start.1
  303.9 21.0 %collective-permute-start.5 = (bf16[160,1280]{1,0:T(8,128)(2,1)S(1)}, bf16[160,1280]{1,0:T(8,128)(2,1)}, u32[]{:S(2)}, u32[]{:S(2)}) collective-permute-start(bf16[160,1280]{1,0:T(8,128)(2,1)S(1)} %collective-permute-done.4), channel_id=1, source_target_pairs={{4,0},{8,4},{12,8},{16,12},{20,16},{24,20},{28,24},{0,28},{5,1},{9... | collective-permute-start | bytes 1228808 | tf_op jit(solution)/shard_map/ppermute | solution.py:166
  314.6 8.5 collective-permute-start.2
  323.2 16.1 %collective-permute-start.3 = (bf16[160,1280]{1,0:T(8,128)(2,1)}, bf16[160,1280]{1,0:T(8,128)(2,1)}, u32[]{:S(2)}, u32[]{:S(2)}) collective-permute-start(bf16[160,1280]{1,0:T(8,128)(2,1)} %collective-permute-done.2), channel_id=1, source_target_pairs={{0,4},{4,8},{8,12},{12,16},{16,20},{20,24},{24,28},{28,0},{1,5},{5... | collective-permute-start | bytes 1228808 | tf_op jit(solution)/shard_map/ppermute | solution.py:161
  324.9 70.7 %collective-permute-start.6 = (bf16[160,1280]{1,0:T(8,128)(2,1)}, bf16[160,1280]{1,0:T(8,128)(2,1)}, u32[]{:S(2)}, u32[]{:S(2)}) collective-permute-start(bf16[160,1280]{1,0:T(8,128)(2,1)} %collective-permute-done.5), channel_id=1, source_target_pairs={{4,0},{8,4},{12,8},{16,12},{20,16},{24,20},{28,24},{0,28},{5,1},{9... | collective-permute-start | bytes 1228808 | tf_op jit(solution)/shard_map/ppermute | solution.py:166
  382.9 208.5 %reduce-scatter.36.cloned.1.call-start = ((), (), s32[]{:S(2)}) async-start(), calls=%async_computation.31 | async-start | bytes 1966080 | tf_op jit(solution)/shard_map/reduce_scatter | solution.py:116
  395.2 249.5 %reduce-scatter.24.cloned.1.call-start = ((), (), s32[]{:S(2)}) async-start(), calls=%async_computation.21 | async-start | bytes 3276800 | tf_op jit(solution)/shard_map/reduce_scatter | solution.py:125
  534.4 164.2 %reduce-scatter.22.cloned.1.call-start = ((), (), s32[]{:S(2)}) async-start(), calls=%async_computation.20 | async-start | bytes 3276800 | tf_op jit(solution)/shard_map/reduce_scatter | solution.py:116
  544.3 193.1 %all-gather.30.cloned.1.call-start = ((), (), s32[]{:S(2)}) async-start(), calls=%async_computation.33 | async-start | bytes 1966080 | tf_op jit(solution)/shard_map/all_gather | solution.py:112
  595.9 197.2 %all-gather.22.cloned.1.call-start = ((), (), s32[]{:S(2)}) async-start(), calls=%async_computation.22 | async-start | bytes 3276800 | tf_op jit(solution)/shard_map/all_gather | solution.py:112
  704.1 211.7 %reduce-scatter.48.cloned.1.call-start = ((), (), s32[]{:S(2)}) async-start(), calls=%async_computation.40 | async-start | bytes 884736
  760.4 157.0 %reduce-scatter.46.cloned.1.call-start = ((), (), s32[]{:S(2)}) async-start(), calls=%async_computation.39 | async-start | bytes 2211840
  778.7 140.7 %reduce-scatter.40.cloned.1.call-start = ((), (), s32[]{:S(2)}) async-start(), calls=%async_computation.34 | async-start | bytes 1966080 | tf_op jit(solution)/shard_map/reduce_scatter | solution.py:125
  782.7 252.8 %all-reduce.30.cloned.1.call-start = ((), (), s32[]{:S(2)}) async-start(), calls=%async_computation.41 | async-start | bytes 15728640
  872.4 217.7 %reduce-scatter.26.cloned.1.call-start = ((), (), s32[]{:S(2)}) async-start(), calls=%async_computation.23 | async-start | bytes 3276800 | tf_op jit(solution)/shard_map/reduce_scatter | solution.py:125
  880.3 256.0 %reduce-scatter.44.cloned.1.call-start = ((), (), s32[]{:S(2)}) async-start(), calls=%async_computation.36 | async-start | bytes 2654208 | tf_op jit(solution)/shard_map/reduce_scatter | solution.py:390
  885.6 297.2 %reduce-scatter.42.cloned.1.call-start = ((), (), s32[]{:S(2)}) async-start(), calls=%async_computation.35 | async-start | bytes 2654208 | tf_op jit(solution)/shard_map/reduce_scatter | solution.py:389
  890.7 359.2 %reduce-scatter.32.cloned.1.call-start = ((), (), s32[]{:S(2)}) async-start(), calls=%async_computation.26 | async-start | bytes 7372800 | tf_op jit(solution)/shard_map/reduce_scatter | solution.py:380
  900.6 416.6 %reduce-scatter.30.cloned.1.call-start = ((), (), s32[]{:S(2)}) async-start(), calls=%async_computation.25 | async-start | bytes 7372800 | tf_op jit(solution)/shard_map/reduce_scatter | solution.py:379
  909.6 451.8 %reduce-scatter.28.cloned.1.call-start = ((), (), s32[]{:S(2)}) async-start(), calls=%async_computation.24 | async-start | bytes 2211840 | tf_op jit(solution)/shard_map/reduce_scatter | solution.py:378
  930.2 163.3 %copy-start.87 = (f32[1280]{0:T(1024)S(1)}, f32[1280]{0:T(1024)}, u32[]{:S(2)}) copy-start(f32[1280]{0:T(1024)} %get-tuple-element.84) | copy-start | bytes 15364
  930.2 163.3 %copy-start.88 = (f32[1280]{0:T(1024)S(1)}, f32[1280]{0:T(1024)}, u32[]{:S(2)}) copy-start(f32[1280]{0:T(1024)} %get-tuple-element.92) | copy-start | bytes 15364
  930.2 163.3 %copy-start.91 = (f32[768]{0:T(1024)S(1)}, f32[768]{0:T(1024)}, u32[]{:S(2)}) copy-start(f32[768]{0:T(1024)} %get-tuple-element.88) | copy-start | bytes 9220
  930.3 203.2 %copy-start.15 = (f32[256,1280]{1,0:T(8,128)S(1)}, f32[256,1280]{1,0:T(8,128)}, u32[]{:S(2)}) copy-start(f32[256,1280]{1,0:T(8,128)} %copy-done.14) | copy-start | bytes 3932164
  930.3 203.2 %copy-start.24 = (bf16[1,256,1280]{2,1,0:T(8,128)(2,1)S(1)}, bf16[1,256,1280]{2,1,0:T(8,128)(2,1)}, u32[]{:S(2)}) copy-start(bf16[1,256,1280]{2,1,0:T(8,128)(2,1)} %param.31) | copy-start | bytes 1966084
  930.3 203.2 %copy-start.96 = (f32[256]{0:T(256)S(1)}, f32[256]{0:T(256)}, u32[]{:S(2)}) copy-start(f32[256]{0:T(256)} %copy-done.95) | copy-start | bytes 3076
  (137 other events, 3536.3 us)
Sparse Core Ops, SparseCore 0:
  51.2 36.5 all-gather.23
  89.9 53.6 all-gather.13
  145.6 30.2 all-gather.15
  178.0 35.2 reduce-scatter.33
  215.5 51.0 reduce-scatter.19
  268.6 36.7 all-gather.25
  307.3 26.8 all-gather.27
  335.7 37.0 all-gather.33
  375.0 53.6 all-gather.17
  430.1 53.5 all-gather.31
  485.6 31.6 all-gather.19
  519.4 35.2 reduce-scatter.37
  557.0 34.2 reduce-scatter.35
  593.5 51.0 reduce-scatter.23
  646.8 51.7 reduce-scatter.21
  700.6 36.7 all-gather.29
  739.4 53.6 all-gather.21
  796.1 33.8 reduce-scatter.47
  833.4 40.2 reduce-scatter.45
  876.0 35.2 reduce-scatter.39
  915.0 120.4 all-reduce.29
  1037.8 52.2 reduce-scatter.25
  1094.0 42.1 reduce-scatter.43
  1140.4 42.4 reduce-scatter.41
  1186.9 63.0 reduce-scatter.31
  1254.2 62.9 reduce-scatter.29
  1321.1 40.2 reduce-scatter.27
